TPU v7x, 32 devices: a whole 2x2x4 slice. The times are simulated.
32 devices in a mesh: chan: 2 (over x), cyl: 4 (over z), tm: 4 (over y, core).
Axes of the slice: x: 2, y: 2, z: 4, core: 2. Of those that a mesh axis runs over, the one named last changes fastest.
Arguments:
- voltages: bfloat16 [8, 4, 2, 2, 256, 2048], P('chan', 'cyl', None, None, None, 'tm'), may hold values from -6 to 6
- feed_gains: float32 [8, 4, 2, 2, 256], P('chan', 'cyl'), may hold values from -8 to 8
- grid_slot: int32 [4, 256], replicated, may hold values from 0 to 511, as said below
- transit_start: int32 [4], replicated, may hold values from 0 to 1024
Outputs:
- beam_map: float32 [8, 4, 512], P('chan', None, ('cyl', 'tm'))
- transit_snr: float32 [4, 4, 512], P(None, None, ('cyl', 'tm'))
Inputs may be any that keep to these rules, and one draw needn't show every extreme that they name: `grid_slot`: within each cylinder the 256 grid points are distinct.
All inputs are finite; a program needn't handle non-finite values.
Results may differ from a plain program's by a relative error of at most 0.0031.
Values may be sent and summed in bfloat16 or wider, within the bound.
A program may use at most 64 MiB of HBM per device.

v0:
```python
import functools
import math

import jax
import jax.numpy as jnp
from jax import lax
from jax.experimental import pallas as pl
from jax.experimental.pallas import tpu as pltpu
from jax.sharding import PartitionSpec as P

NS = 512
EPSILON = 1e-06
MESH = pl.DeviceIdType.MESH
LANES = 128


def slot_tables(slots, rows, size):
    turns = (slots * rows) & (size - 1)
    eighth = size // 8
    quarter = size // 4
    quadrant = (turns + eighth) // quarter
    rest = turns - quadrant * quarter
    x = rest.astype(jnp.float32) * (2.0 * math.pi / size)
    x2 = x * x
    sine = x * (1.0 + x2 * (-1.0 / 6 + x2 * (1.0 / 120 + x2 * (-1.0 / 5040 + x2 * (1.0 / 362880)))))
    cosine = 1.0 + x2 * (-0.5 + x2 * (1.0 / 24 + x2 * (-1.0 / 720 + x2 * (1.0 / 40320))))
    odd = (quadrant & 1) == 1
    c = jnp.where(odd, sine, cosine)
    s = jnp.where(odd, cosine, sine)
    c = jnp.where((quadrant == 1) | (quadrant == 2), -c, c)
    s = jnp.where((quadrant == 2) | (quadrant == 3), -s, s)
    return c, s


def kernel(
    sizes,
    volt,
    gains,
    slots,
    starts,
    map_out,
    snr_out,
    vbuf,
    gbuf,
    gwide,
    table,
    cal,
    spec,
    acc,
    shapes,
    mom_send,
    mom_recv,
    pool_send,
    pool_recv,
    vs_sem,
    vr_sem,
    gs_sem,
    gr_sem,
    ms_sem,
    mr_sem,
    ps_sem,
    pr_sem,
):
    nchan, ncyl, ntm, ch_dev, fr_dev, pols, feeds, ncal = sizes
    chunks = fr_dev // LANES
    frames = fr_dev * ntm
    window = frames // 2
    channels = ch_dev * nchan
    owners = ncyl * ntm
    my_chan = lax.axis_index("chan")
    me = lax.axis_index("cyl")
    my_tm = lax.axis_index("tm")
    mine = me * ntm + my_tm

    near = me + 1 - 2 * (me % 2)
    middle = (me + 2) % ncyl
    mirror = ncyl - 1 - me
    peers = (near, mirror, middle)

    def owner_device(step):
        target = (mine + step) % owners
        return target, {"cyl": target // ntm, "tm": target % ntm}

    def chan_device(step):
        target = (my_chan + step) % nchan
        return target, {"chan": target}

    barrier = pltpu.get_barrier_semaphore()
    for step in range(1, owners):
        pl.semaphore_signal(barrier, inc=1, device_id=owner_device(step)[1], device_id_type=MESH)
    for step in range(1, nchan):
        pl.semaphore_signal(barrier, inc=1, device_id=chan_device(step)[1], device_id_type=MESH)
    pl.semaphore_wait(barrier, owners - 1 + nchan - 1)

    def gain_copy(j):
        return pltpu.make_async_remote_copy(
            src_ref=gains.at[peers[j], 0],
            dst_ref=gbuf.at[me],
            send_sem=gs_sem.at[j],
            recv_sem=gr_sem.at[me],
            device_id={"cyl": peers[j]},
            device_id_type=MESH,
        )

    def volt_copy(j, k):
        return pltpu.make_async_remote_copy(
            src_ref=volt.at[peers[j], 0, :, :, :, pl.ds(k * LANES, LANES)],
            dst_ref=vbuf.at[k, me],
            send_sem=vs_sem.at[j, k],
            recv_sem=vr_sem.at[k, me],
            device_id={"cyl": peers[j]},
            device_id_type=MESH,
        )

    def own_volt(k):
        return pltpu.make_async_copy(
            volt.at[me, 0, :, :, :, pl.ds(k * LANES, LANES)], vbuf.at[k, me], vr_sem.at[k, me]
        )

    own_gain = pltpu.make_async_copy(gains.at[me, 0], gbuf.at[me], gr_sem.at[me])

    for j in range(3):
        gain_copy(j).start()
    own_gain.start()
    for k in range(chunks):
        volt_copy(0, k).start()
    for k in range(chunks):
        volt_copy(1, k).start()
        volt_copy(2, k).start()
    for k in range(chunks):
        own_volt(k).start()

    rows_per = 64

    def build(c, carry):
        slot_row = slots[pl.ds(c, 1), :]

        def block(b, inner):
            base = pl.multiple_of(b * rows_per, rows_per)
            row = lax.broadcasted_iota(jnp.int32, (rows_per, feeds), 0) + base
            cosine, sine = slot_tables(slot_row, row, NS)
            factor = 1.0 / math.sqrt(feeds)
            cosine = (cosine * factor).astype(jnp.bfloat16)
            sine = (sine * factor).astype(jnp.bfloat16)
            table[c, pl.ds(base, rows_per), pl.ds(0, feeds)] = cosine
            table[c, pl.ds(base, rows_per), pl.ds(feeds, feeds)] = sine
            low = pl.multiple_of(base + NS, rows_per)
            table[c, pl.ds(low, rows_per), pl.ds(0, feeds)] = -sine
            table[c, pl.ds(low, rows_per), pl.ds(feeds, feeds)] = cosine
            return inner

        return lax.fori_loop(0, NS // rows_per, block, carry)

    lax.fori_loop(0, ncyl, build, 0)

    def template(first, width, k):
        frame = lax.broadcasted_iota(jnp.int32, (8, width), 1) + first
        relative = frame - starts[k]
        inside = (relative >= 0) & (relative < window)
        wave = jnp.sin(math.pi * (relative.astype(jnp.float32) + 0.5) / window)
        return jnp.where(inside, wave * wave, 0.0)

    tsum = []
    tsq = []
    for k in range(ncal):
        whole = template(0, frames, k)[0:1, :]
        tsum.append(jnp.sum(whole, axis=1, keepdims=True))
        tsq.append(jnp.sum(whole * whole, axis=1, keepdims=True))
        own = template(my_tm * fr_dev, fr_dev, k)
        for t in range(chunks):
            shapes[t, k] = own[:, t * LANES : (t + 1) * LANES]

    acc[...] = jnp.zeros_like(acc)

    for j in range(3):
        gain_copy(j).wait_send()
        pltpu.make_async_remote_copy(
            src_ref=gains.at[peers[j], 0],
            dst_ref=gbuf.at[peers[j]],
            send_sem=gs_sem.at[j],
            recv_sem=gr_sem.at[peers[j]],
            device_id={"cyl": peers[j]},
            device_id_type=MESH,
        ).wait_recv()
    own_gain.wait()
    flat = jnp.concatenate([gbuf[c, p] for c in range(ncyl) for p in range(pols)], axis=0)
    tall = flat.T
    for i in range(ncyl * pols * 2):
        gwide[i] = jnp.broadcast_to(tall[:, i : i + 1], (feeds, LANES))

    def chunk_step(k, carry):
        for j in range(3):
            pltpu.make_async_remote_copy(
                src_ref=volt.at[peers[j], 0, :, :, :, pl.ds(0, LANES)],
                dst_ref=vbuf.at[k, peers[j]],
                send_sem=vs_sem.at[j, k],
                recv_sem=vr_sem.at[k, peers[j]],
                device_id={"cyl": peers[j]},
                device_id_type=MESH,
            ).wait_recv()
        own_volt(k).wait()

        def form(i, inner):
            c = i // pols
            p = i % pols
            gain_re = gwide[2 * i]
            gain_im = gwide[2 * i + 1]
            volt_re = vbuf[k, c, p, 0].astype(jnp.float32)
            volt_im = vbuf[k, c, p, 1].astype(jnp.float32)
            cal[0:feeds, :] = (gain_re * volt_re - gain_im * volt_im).astype(jnp.bfloat16)
            cal[feeds : 2 * feeds, :] = (gain_re * volt_im + gain_im * volt_re).astype(jnp.bfloat16)
            spec[i] = jnp.dot(table[c], cal[...], preferred_element_type=jnp.float32).astype(
                jnp.bfloat16
            )
            return inner

        lax.fori_loop(0, ncyl * pols, form, 0)

        rows = 16
        span = NS // owners

        def beams(b, inner):
            base = pl.multiple_of(b * rows, rows)
            owner = b // (span // rows)
            part = (b % (span // rows)) * rows
            power = [None] * 4
            for p in range(pols):
                re = []
                im = []
                for c in range(4):
                    re.append(spec[c * pols + p, pl.ds(base, rows), :].astype(jnp.float32))
                    low = pl.multiple_of(base + NS, rows)
                    im.append(spec[c * pols + p, pl.ds(low, rows), :].astype(jnp.float32))
                re_even, re_odd = re[0] + re[2], re[1] + re[3]
                im_even, im_odd = im[0] + im[2], im[1] + im[3]
                re_alt, im_alt = re[0] - re[2], im[0] - im[2]
                re_skew, im_skew = re[1] - re[3], im[1] - im[3]
                formed = (
                    (re_even + re_odd, im_even + im_odd),
                    (re_alt + im_skew, im_alt - re_skew),
                    (re_even - re_odd, im_even - im_odd),
                    (re_alt - im_skew, im_alt + re_skew),
                )
                for e in range(4):
                    square = formed[e][0] * formed[e][0] + formed[e][1] * formed[e][1]
                    power[e] = square if power[e] is None else power[e] + square
            for e in range(4):
                value = 0.25 * power[e]
                where = pl.ds(pl.multiple_of(e * span + part, rows), rows)
                acc[0, owner, where, :] += value
                acc[1, owner, where, :] += value * value
                for t in range(ncal):
                    shape = shapes[k, t]
                    acc[2 + t, owner, where, :] += value * jnp.concatenate([shape, shape], axis=0)
            return inner

        return lax.fori_loop(0, NS // rows, beams, carry)

    lax.fori_loop(0, chunks, chunk_step, 0)

    lane = lax.broadcasted_iota(jnp.int32, (LANES, LANES), 1)

    def gather(d, carry):
        merged = jnp.zeros((LANES, LANES), jnp.float32)
        for i in range(2 + ncal):
            total = jnp.sum(acc[i, d], axis=1, keepdims=True)
            merged = jnp.where(lane == i, total, merged)
        mom_send[d] = merged.T[0:8, :]
        return carry

    lax.fori_loop(0, owners, gather, 0)

    def moment_copy(step, target, place, device):
        return pltpu.make_async_remote_copy(
            src_ref=mom_send.at[target],
            dst_ref=mom_recv.at[place],
            send_sem=ms_sem.at[step],
            recv_sem=mr_sem.at[place],
            device_id=device,
            device_id_type=MESH,
        )

    for step in range(1, owners):
        target, device = owner_device(step)
        moment_copy(step, target, mine, device).start()
    own_moment = pltpu.make_async_copy(mom_send.at[mine], mom_recv.at[mine], mr_sem.at[mine])
    own_moment.start()
    for step in range(1, owners):
        target, device = owner_device(step)
        moment_copy(step, target, target, device).wait_recv()
    own_moment.wait()

    pooled = jnp.zeros((8, LANES), jnp.float32)
    for z in range(ncyl):
        own = mom_recv[z * ntm]
        for t in range(1, ntm):
            own = own + mom_recv[z * ntm + t]
        map_out[z : z + 1, :] = own[0:1, :] / frames
        pooled = pooled + own
    pool_send[...] = pooled

    def pool_copy(step, place, device):
        return pltpu.make_async_remote_copy(
            src_ref=pool_send,
            dst_ref=pool_recv.at[place],
            send_sem=ps_sem.at[step],
            recv_sem=pr_sem.at[place],
            device_id=device,
            device_id_type=MESH,
        )

    for step in range(1, nchan):
        target, device = chan_device(step)
        pool_copy(step, my_chan, device).start()
    for step in range(1, nchan):
        target, device = chan_device(step)
        pool_copy(step, target, device).wait_recv()
        pooled = pooled + pool_recv[target]

    samples = channels * frames
    zeroth = pooled[0:1, :]
    average = zeroth / samples
    variance = pooled[1:2, :] / samples - average * average
    for k in range(ncal):
        spread = channels * (tsq[k] - tsum[k] * tsum[k] / frames)
        numerator = pooled[2 + k : 3 + k, :] - tsum[k] * zeroth / frames
        snr_out[k : k + 1, :] = numerator / jnp.sqrt(spread * (variance + EPSILON))

    for j in range(3):
        for k in range(chunks):
            volt_copy(j, k).wait_send()
    for step in range(1, owners):
        target, device = owner_device(step)
        moment_copy(step, target, mine, device).wait_send()
    for step in range(1, nchan):
        target, device = chan_device(step)
        pool_copy(step, my_chan, device).wait_send()


def per_device(voltages, feed_gains, grid_slot, transit_start):
    ch_dev, _, pols, _, feeds, fr_dev = voltages.shape
    nchan = lax.axis_size("chan")
    ncyl = lax.axis_size("cyl")
    ntm = lax.axis_size("tm")
    ncal = transit_start.shape[0]
    assert ncyl == 4 and ch_dev == ncyl
    chunks = fr_dev // LANES
    owners = ncyl * ntm
    sizes = (nchan, ncyl, ntm, ch_dev, fr_dev, pols, feeds, ncal)
    dma = pltpu.SemaphoreType.DMA
    f32 = jnp.float32
    bf16 = jnp.bfloat16
    beam_map, transit_snr = pl.pallas_call(
        functools.partial(kernel, sizes),
        out_shape=(
            jax.ShapeDtypeStruct((ch_dev, LANES), f32),
            jax.ShapeDtypeStruct((ncal, LANES), f32),
        ),
        in_specs=[
            pl.BlockSpec(memory_space=pl.ANY),
            pl.BlockSpec(memory_space=pl.ANY),
            pl.BlockSpec(memory_space=pltpu.VMEM),
            pl.BlockSpec(memory_space=pltpu.SMEM),
        ],
        out_specs=(
            pl.BlockSpec(memory_space=pltpu.VMEM),
            pl.BlockSpec(memory_space=pltpu.VMEM),
        ),
        scratch_shapes=[
            pltpu.VMEM((chunks, ncyl, pols, 2, feeds, LANES), bf16),
            pltpu.VMEM((ncyl, pols, 2, feeds), f32),
            pltpu.VMEM((ncyl * pols * 2, feeds, LANES), f32),
            pltpu.VMEM((ncyl, 2 * NS, 2 * feeds), bf16),
            pltpu.VMEM((2 * feeds, LANES), bf16),
            pltpu.VMEM((ncyl * pols, 2 * NS, LANES), bf16),
            pltpu.VMEM((2 + ncal, owners, 4 * NS // owners, LANES), f32),
            pltpu.VMEM((chunks, ncal, 8, LANES), f32),
            pltpu.VMEM((owners, 8, LANES), f32),
            pltpu.VMEM((owners, 8, LANES), f32),
            pltpu.VMEM((8, LANES), f32),
            pltpu.VMEM((nchan, 8, LANES), f32),
            dma((3, chunks)),
            dma((chunks, ncyl)),
            dma((3,)),
            dma((ncyl,)),
            dma((owners,)),
            dma((owners,)),
            dma((nchan,)),
            dma((nchan,)),
        ],
        compiler_params=pltpu.CompilerParams(
            collective_id=0, has_side_effects=True, vmem_limit_bytes=60 * 1024 * 1024
        ),
    )(voltages, feed_gains, grid_slot, transit_start)
    span = NS // owners
    return (
        beam_map.reshape(ch_dev, 4, span),
        transit_snr.reshape(ncal, 4, span),
    )


def solution(mesh):
    in_specs = (
        P("chan", "cyl", None, None, None, "tm"),
        P("chan", "cyl", None, None, None),
        P(),
        P(),
    )
    out_specs = (P("chan", None, ("cyl", "tm")), P(None, None, ("cyl", "tm")))
    return jax.shard_map(
        per_device, mesh=mesh, in_specs=in_specs, out_specs=out_specs, check_vma=False
    )
```

profile of v0, /device:TPU:0, one launch (start us, length us, event | category | flops | bytes accessed | tf_op | source)
XLA Modules:
  0.0 119.3 jit_solution(15408207623771062633)
XLA Ops:
  0.6 116.0 %shard_map.59 = (f32[4,128]{1,0:T(4,128)}, f32[4,128]{1,0:T(4,128)}) custom-call(bf16[4,1,2,2,256,512]{5,4,3,2,1,0:T(8,128)(2,1)} %volt.1, f32[4,1,2,2,256]{4,3,2,1,0:T(2,128)} %gains.1, s32[4,256]{1,0:T(4,128)} %slots.1, s32[4]{0:T(128)} %starts.1), custom_call_target="tpu_custom_call" | custom-call | tf_op jit(solution)/shard_map/pallas_call | solution.py:353
  116.6 1.4 %reshape.10 = f32[4,4,32]{2,1,0:T(4,128)} reshape(f32[4,128]{1,0:T(4,128)} %get-tuple-element.4) | data formatting | bytes 4096 | tf_op jit(solution)/shard_map/reshape | solution.py:397
  118.0 1.3 %reshape.11 = f32[4,4,32]{2,1,0:T(4,128)} reshape(f32[4,128]{1,0:T(4,128)} %get-tuple-element.5) | data formatting | bytes 4096 | tf_op jit(solution)/shard_map/reshape | solution.py:398
where the time goes:
time: 120 us; the launch traced here: 119 us
  Pallas kernels  116 us (97%)
  local copies, waits for them, and re-layouts  2.68 us (2%)
    pallas_call x1, Pallas kernels, per_device(): pl.pallas_call(functools.partial(kernel, sizes), out_shape=(jax.ShapeDtyp...  116 us

commit v1 on v0

--- a/solution.py
+++ b/solution.py
@@ -102,19 +102,21 @@
             device_id_type=MESH,
         )
 
-    def volt_copy(j, k):
+    def volt_copy(j, k, p, sender):
         return pltpu.make_async_remote_copy(
-            src_ref=volt.at[peers[j], 0, :, :, :, pl.ds(k * LANES, LANES)],
-            dst_ref=vbuf.at[k, me],
-            send_sem=vs_sem.at[j, k],
-            recv_sem=vr_sem.at[k, me],
+            src_ref=volt.at[peers[j], 0, p, :, :, pl.ds(k * LANES, LANES)],
+            dst_ref=vbuf.at[k, p, sender],
+            send_sem=vs_sem.at[j, k, p],
+            recv_sem=vr_sem.at[k, p, sender],
             device_id={"cyl": peers[j]},
             device_id_type=MESH,
         )
 
-    def own_volt(k):
+    def own_volt(k, p):
         return pltpu.make_async_copy(
-            volt.at[me, 0, :, :, :, pl.ds(k * LANES, LANES)], vbuf.at[k, me], vr_sem.at[k, me]
+            volt.at[me, 0, p, :, :, pl.ds(k * LANES, LANES)],
+            vbuf.at[k, p, me],
+            vr_sem.at[k, p, me],
         )
 
     own_gain = pltpu.make_async_copy(gains.at[me, 0], gbuf.at[me], gr_sem.at[me])
@@ -122,13 +124,14 @@
     for j in range(3):
         gain_copy(j).start()
     own_gain.start()
-    for k in range(chunks):
-        volt_copy(0, k).start()
-    for k in range(chunks):
-        volt_copy(1, k).start()
-        volt_copy(2, k).start()
-    for k in range(chunks):
-        own_volt(k).start()
+    pieces = [(k, p) for k in range(chunks) for p in range(pols)]
+    for k, p in pieces:
+        volt_copy(0, k, p, me).start()
+    for k, p in pieces:
+        volt_copy(2, k, p, me).start()
+        volt_copy(1, k, p, me).start()
+    for k, p in pieces:
+        own_volt(k, p).start()
 
     rows_per = 64
 
@@ -189,32 +192,27 @@
         gwide[i] = jnp.broadcast_to(tall[:, i : i + 1], (feeds, LANES))
 
     def chunk_step(k, carry):
-        for j in range(3):
-            pltpu.make_async_remote_copy(
-                src_ref=volt.at[peers[j], 0, :, :, :, pl.ds(0, LANES)],
-                dst_ref=vbuf.at[k, peers[j]],
-                send_sem=vs_sem.at[j, k],
-                recv_sem=vr_sem.at[k, peers[j]],
-                device_id={"cyl": peers[j]},
-                device_id_type=MESH,
-            ).wait_recv()
-        own_volt(k).wait()
-
-        def form(i, inner):
-            c = i // pols
-            p = i % pols
+        def form(c, p, k):
+            i = c * pols + p
             gain_re = gwide[2 * i]
             gain_im = gwide[2 * i + 1]
-            volt_re = vbuf[k, c, p, 0].astype(jnp.float32)
-            volt_im = vbuf[k, c, p, 1].astype(jnp.float32)
+            volt_re = vbuf[k, p, c, 0].astype(jnp.float32)
+            volt_im = vbuf[k, p, c, 1].astype(jnp.float32)
             cal[0:feeds, :] = (gain_re * volt_re - gain_im * volt_im).astype(jnp.bfloat16)
             cal[feeds : 2 * feeds, :] = (gain_re * volt_im + gain_im * volt_re).astype(jnp.bfloat16)
             spec[i] = jnp.dot(table[c], cal[...], preferred_element_type=jnp.float32).astype(
                 jnp.bfloat16
             )
+
+        def form_pol(p, inner):
+            own_volt(k, p).wait()
+            form(me, p, k)
+            for j in (0, 2, 1):
+                volt_copy(j, k, p, peers[j]).wait_recv()
+                form(peers[j], p, k)
             return inner
 
-        lax.fori_loop(0, ncyl * pols, form, 0)
+        lax.fori_loop(0, pols, form_pol, 0)
 
         rows = 16
         span = NS // owners
@@ -254,7 +252,7 @@
                     acc[2 + t, owner, where, :] += value * jnp.concatenate([shape, shape], axis=0)
             return inner
 
-        return lax.fori_loop(0, NS // rows, beams, carry)
+        return lax.fori_loop(0, NS // rows, beams, carry, unroll=2)
 
     lax.fori_loop(0, chunks, chunk_step, 0)
 
@@ -268,7 +266,7 @@
         mom_send[d] = merged.T[0:8, :]
         return carry
 
-    lax.fori_loop(0, owners, gather, 0)
+    lax.fori_loop(0, owners, gather, 0, unroll=True)
 
     def moment_copy(step, target, place, device):
         return pltpu.make_async_remote_copy(
@@ -327,14 +325,21 @@
         snr_out[k : k + 1, :] = numerator / jnp.sqrt(spread * (variance + EPSILON))
 
     for j in range(3):
-        for k in range(chunks):
-            volt_copy(j, k).wait_send()
+        for k, p in pieces:
+            volt_copy(j, k, p, me).wait_send()
     for step in range(1, owners):
         target, device = owner_device(step)
         moment_copy(step, target, mine, device).wait_send()
     for step in range(1, nchan):
         target, device = chan_device(step)
         pool_copy(step, my_chan, device).wait_send()
+
+
+def place_outputs(map_in, snr_in, map_out, snr_out):
+    width = map_out.shape[2]
+    for e in range(map_out.shape[1]):
+        map_out[:, e, :] = map_in[:, e * width : (e + 1) * width]
+        snr_out[:, e, :] = snr_in[:, e * width : (e + 1) * width]
 
 
 def per_device(voltages, feed_gains, grid_slot, transit_start):
@@ -367,7 +372,7 @@
             pl.BlockSpec(memory_space=pltpu.VMEM),
         ),
         scratch_shapes=[
-            pltpu.VMEM((chunks, ncyl, pols, 2, feeds, LANES), bf16),
+            pltpu.VMEM((chunks, pols, ncyl, 2, feeds, LANES), bf16),
             pltpu.VMEM((ncyl, pols, 2, feeds), f32),
             pltpu.VMEM((ncyl * pols * 2, feeds, LANES), f32),
             pltpu.VMEM((ncyl, 2 * NS, 2 * feeds), bf16),
@@ -379,8 +384,8 @@
             pltpu.VMEM((owners, 8, LANES), f32),
             pltpu.VMEM((8, LANES), f32),
             pltpu.VMEM((nchan, 8, LANES), f32),
-            dma((3, chunks)),
-            dma((chunks, ncyl)),
+            dma((3, chunks, pols)),
+            dma((chunks, pols, ncyl)),
             dma((3,)),
             dma((ncyl,)),
             dma((owners,)),
@@ -393,10 +398,16 @@
         ),
     )(voltages, feed_gains, grid_slot, transit_start)
     span = NS // owners
-    return (
-        beam_map.reshape(ch_dev, 4, span),
-        transit_snr.reshape(ncal, 4, span),
-    )
+    vmem = pl.BlockSpec(memory_space=pltpu.VMEM)
+    return pl.pallas_call(
+        place_outputs,
+        out_shape=(
+            jax.ShapeDtypeStruct((ch_dev, 4, span), f32),
+            jax.ShapeDtypeStruct((ncal, 4, span), f32),
+        ),
+        in_specs=[vmem, vmem],
+        out_specs=(vmem, vmem),
+    )(beam_map, transit_snr)
 
 
 def solution(mesh):

time: 120 us -> 113 us (0.942)
  Pallas kernels: 116 us -> 112 us
  local copies, waits for them, and re-layouts: 2.68 us -> 0 us
    pallas_call x1, Pallas kernels: 116 us -> 111 us  [per_device(): pl.pallas_call(functools.partial(kernel, sizes), out_shape=(jax.ShapeDtyp...]
    reshape x2 -> x0, local copies, waits for them, and re-layouts: 2.68 us -> none  [the longest x1 1.35 us: per_device(): beam_map.reshape(ch_dev, 4, span)]
    pallas_call x0 -> x1, Pallas kernels: none -> 1.37 us  [per_device(): pl.pallas_call(place_outputs, out_shape=(jax.ShapeDtypeStruct((ch_dev, 4,...]
where the time goes in v1:
time: 113 us
  Pallas kernels  112 us (99%)
    pallas_call x1, Pallas kernels, per_device(): pl.pallas_call(functools.partial(kernel, sizes), out_shape=(jax.ShapeDtyp...  111 us

profile of v1, /device:TPU:0, one launch (start us, length us, event | category | flops | bytes accessed | tf_op | source)
XLA Modules:
  0.0 112.8 jit_solution(11558490457508008788)
XLA Ops:
  0.6 110.8 %shard_map.59 = (f32[4,128]{1,0:T(4,128)}, f32[4,128]{1,0:T(4,128)}) custom-call(bf16[4,1,2,2,256,512]{5,4,3,2,1,0:T(8,128)(2,1)} %volt.1, f32[4,1,2,2,256]{4,3,2,1,0:T(2,128)} %gains.1, s32[4,256]{1,0:T(4,128)} %slots.1, s32[4]{0:T(128)} %starts.1), custom_call_target="tpu_custom_call" | custom-call | tf_op jit(solution)/shard_map/pallas_call | solution.py:358
  111.5 1.4 %shard_map.60 = (f32[4,4,32]{2,1,0:T(4,128)}, f32[4,4,32]{2,1,0:T(4,128)}) custom-call(f32[4,128]{1,0:T(4,128)} %get-tuple-element.4.map_in, f32[4,128]{1,0:T(4,128)} %get-tuple-element.5.snr_in), custom_call_target="tpu_custom_call" | custom-call | tf_op jit(solution)/shard_map/pallas_call | solution.py:402

commit v2 on v1

--- a/solution.py
+++ b/solution.py
@@ -60,6 +60,7 @@
     mr_sem,
     ps_sem,
     pr_sem,
+    hop_sem,
 ):
     nchan, ncyl, ntm, ch_dev, fr_dev, pols, feeds, ncal = sizes
     chunks = fr_dev // LANES
@@ -77,20 +78,33 @@
     mirror = ncyl - 1 - me
     peers = (near, mirror, middle)
 
-    def owner_device(step):
-        target = (mine + step) % owners
-        return target, {"cyl": target // ntm, "tm": target % ntm}
+    others = []
+    for z in (mirror, middle, near, me):
+        for dt in range(1 if z is me else 0, ntm):
+            t = (my_tm + dt) % ntm
+            others.append((z * ntm + t, {"cyl": z, "tm": t}))
 
     def chan_device(step):
         target = (my_chan + step) % nchan
         return target, {"chan": target}
 
+    inner = (me == 1) | (me == 2)
+    inward = jnp.where(me < 2, me + 1, me - 1)
+
     barrier = pltpu.get_barrier_semaphore()
-    for step in range(1, owners):
-        pl.semaphore_signal(barrier, inc=1, device_id=owner_device(step)[1], device_id_type=MESH)
+    pl.semaphore_signal(barrier, inc=1, device_id={"cyl": inward}, device_id_type=MESH)
+
+    @pl.when(inner)
+    def _():
+        pl.semaphore_signal(barrier, inc=1, device_id={"cyl": near}, device_id_type=MESH)
+
+    for step in range(1, ntm):
+        pl.semaphore_signal(
+            barrier, inc=1, device_id={"tm": (my_tm + step) % ntm}, device_id_type=MESH
+        )
     for step in range(1, nchan):
         pl.semaphore_signal(barrier, inc=1, device_id=chan_device(step)[1], device_id_type=MESH)
-    pl.semaphore_wait(barrier, owners - 1 + nchan - 1)
+    pl.semaphore_wait(barrier, jnp.where(inner, 2, 1) + ntm - 1 + nchan - 1)
 
     def gain_copy(j):
         return pltpu.make_async_remote_copy(
@@ -121,13 +135,45 @@
 
     own_gain = pltpu.make_async_copy(gains.at[me, 0], gbuf.at[me], gr_sem.at[me])
 
-    for j in range(3):
-        gain_copy(j).start()
+    pieces = [(k, p) for k in range(chunks) for p in range(pols)]
+    gain_copy(0).start()
     own_gain.start()
-    pieces = [(k, p) for k in range(chunks) for p in range(pols)]
     for k, p in pieces:
         volt_copy(0, k, p, me).start()
-    for k, p in pieces:
+
+    @pl.when(inner)
+    def _():
+        for p in range(pols):
+            volt_copy(1, 0, p, me).start()
+
+    pl.semaphore_signal(hop_sem.at[0], inc=1, device_id={"cyl": inward}, device_id_type=MESH)
+
+    @pl.when(inner)
+    def _():
+        pl.semaphore_signal(hop_sem.at[0], inc=1, device_id={"cyl": near}, device_id_type=MESH)
+        pl.semaphore_wait(hop_sem.at[0], 2)
+        pl.semaphore_signal(hop_sem.at[1], inc=1, device_id={"cyl": near}, device_id_type=MESH)
+
+    @pl.when(jnp.logical_not(inner))
+    def _():
+        pl.semaphore_wait(hop_sem.at[0], 1)
+        pl.semaphore_wait(hop_sem.at[1], 1)
+
+    gain_copy(1).start()
+    gain_copy(2).start()
+
+    @pl.when(jnp.logical_not(inner))
+    def _():
+        for p in range(pols):
+            volt_copy(2, 0, p, me).start()
+            volt_copy(1, 0, p, me).start()
+
+    @pl.when(inner)
+    def _():
+        for p in range(pols):
+            volt_copy(2, 0, p, me).start()
+
+    for k, p in pieces[pols:]:
         volt_copy(2, k, p, me).start()
         volt_copy(1, k, p, me).start()
     for k, p in pieces:
@@ -278,13 +324,11 @@
             device_id_type=MESH,
         )
 
-    for step in range(1, owners):
-        target, device = owner_device(step)
+    for step, (target, device) in enumerate(others):
         moment_copy(step, target, mine, device).start()
     own_moment = pltpu.make_async_copy(mom_send.at[mine], mom_recv.at[mine], mr_sem.at[mine])
     own_moment.start()
-    for step in range(1, owners):
-        target, device = owner_device(step)
+    for step, (target, device) in enumerate(others):
         moment_copy(step, target, target, device).wait_recv()
     own_moment.wait()
 
@@ -327,8 +371,7 @@
     for j in range(3):
         for k, p in pieces:
             volt_copy(j, k, p, me).wait_send()
-    for step in range(1, owners):
-        target, device = owner_device(step)
+    for step, (target, device) in enumerate(others):
         moment_copy(step, target, mine, device).wait_send()
     for step in range(1, nchan):
         target, device = chan_device(step)
@@ -392,6 +435,7 @@
             dma((owners,)),
             dma((nchan,)),
             dma((nchan,)),
+            pltpu.SemaphoreType.REGULAR((2,)),
         ],
         compiler_params=pltpu.CompilerParams(
             collective_id=0, has_side_effects=True, vmem_limit_bytes=60 * 1024 * 1024

time: 113 us -> 112 us (level)
    pallas_call x1, Pallas kernels: 111 us -> 109 us  [per_device(): pl.pallas_call(functools.partial(kernel, sizes), out_shape=(jax.ShapeDtyp...]
where the time goes in v2:
time: 112 us; the launch traced here: 111 us
  Pallas kernels  111 us (99%)
    pallas_call x1, Pallas kernels, per_device(): pl.pallas_call(functools.partial(kernel, sizes), out_shape=(jax.ShapeDtyp...  109 us

profile of v2, /device:TPU:0, one launch (start us, length us, event | category | flops | bytes accessed | tf_op | source)
XLA Modules:
  0.0 111.5 jit_solution(17547342087813573347)
XLA Ops:
  0.6 109.5 %shard_map.59 = (f32[4,128]{1,0:T(4,128)}, f32[4,128]{1,0:T(4,128)}) custom-call(bf16[4,1,2,2,256,512]{5,4,3,2,1,0:T(8,128)(2,1)} %volt.1, f32[4,1,2,2,256]{4,3,2,1,0:T(2,128)} %gains.1, s32[4,256]{1,0:T(4,128)} %slots.1, s32[4]{0:T(128)} %starts.1), custom_call_target="tpu_custom_call" | custom-call | tf_op jit(solution)/shard_map/pallas_call | solution.py:401
  110.1 1.4 %shard_map.60 = (f32[4,4,32]{2,1,0:T(4,128)}, f32[4,4,32]{2,1,0:T(4,128)}) custom-call(f32[4,128]{1,0:T(4,128)} %get-tuple-element.4.map_in, f32[4,128]{1,0:T(4,128)} %get-tuple-element.5.snr_in), custom_call_target="tpu_custom_call" | custom-call | tf_op jit(solution)/shard_map/pallas_call | solution.py:446

commit v3 on v2

--- a/solution.py
+++ b/solution.py
@@ -332,12 +332,13 @@
         moment_copy(step, target, target, device).wait_recv()
     own_moment.wait()
 
+    sums = []
     pooled = jnp.zeros((8, LANES), jnp.float32)
     for z in range(ncyl):
         own = mom_recv[z * ntm]
         for t in range(1, ntm):
             own = own + mom_recv[z * ntm + t]
-        map_out[z : z + 1, :] = own[0:1, :] / frames
+        sums.append(own)
         pooled = pooled + own
     pool_send[...] = pooled
 
@@ -354,6 +355,13 @@
     for step in range(1, nchan):
         target, device = chan_device(step)
         pool_copy(step, my_chan, device).start()
+    for z in range(ncyl):
+        map_out[z : z + 1, :] = sums[z][0:1, :] / frames
+    for j in range(3):
+        for k, p in pieces:
+            volt_copy(j, k, p, me).wait_send()
+    for step, (target, device) in enumerate(others):
+        moment_copy(step, target, mine, device).wait_send()
     for step in range(1, nchan):
         target, device = chan_device(step)
         pool_copy(step, target, device).wait_recv()
@@ -368,11 +376,6 @@
         numerator = pooled[2 + k : 3 + k, :] - tsum[k] * zeroth / frames
         snr_out[k : k + 1, :] = numerator / jnp.sqrt(spread * (variance + EPSILON))
 
-    for j in range(3):
-        for k, p in pieces:
-            volt_copy(j, k, p, me).wait_send()
-    for step, (target, device) in enumerate(others):
-        moment_copy(step, target, mine, device).wait_send()
     for step in range(1, nchan):
         target, device = chan_device(step)
         pool_copy(step, my_chan, device).wait_send()

time: 112 us -> 112 us (level)
  no operation moved by 1% of the time
where the time goes in v3:
time: 112 us; the launch traced here: 111 us
  Pallas kernels  111 us (99%)
    pallas_call x1, Pallas kernels, per_device(): pl.pallas_call(functools.partial(kernel, sizes), out_shape=(jax.ShapeDtyp...  109 us

profile of v3, /device:TPU:0, one launch (start us, length us, event | category | flops | bytes accessed | tf_op | source)
XLA Modules:
  0.0 111.4 jit_solution(5044551544657433249)
XLA Ops:
  0.6 109.4 %shard_map.59 = (f32[4,128]{1,0:T(4,128)}, f32[4,128]{1,0:T(4,128)}) custom-call(bf16[4,1,2,2,256,512]{5,4,3,2,1,0:T(8,128)(2,1)} %volt.1, f32[4,1,2,2,256]{4,3,2,1,0:T(2,128)} %gains.1, s32[4,256]{1,0:T(4,128)} %slots.1, s32[4]{0:T(128)} %starts.1), custom_call_target="tpu_custom_call" | custom-call | tf_op jit(solution)/shard_map/pallas_call | solution.py:404
  110.0 1.4 %shard_map.60 = (f32[4,4,32]{2,1,0:T(4,128)}, f32[4,4,32]{2,1,0:T(4,128)}) custom-call(f32[4,128]{1,0:T(4,128)} %get-tuple-element.4.map_in, f32[4,128]{1,0:T(4,128)} %get-tuple-element.5.snr_in), custom_call_target="tpu_custom_call" | custom-call | tf_op jit(solution)/shard_map/pallas_call | solution.py:449
